TPU v7x, 32 devices: a whole 2x2x4 slice. The times are simulated.
32 devices in a mesh: gy: 4 (over y, x), gz: 8 (over z, core).
Axes of the slice: x: 2, y: 2, z: 4, core: 2. Of those that a mesh axis runs over, the one named last changes fastest.
Arguments:
- conduct: float32 [64, 256, 128], P('gy', 'gz'), may hold values from 0.3 to 3
- seeds: int32 [64, 256, 128], P('gy', 'gz'), may hold values 0 or 1
- labels: int32 [64, 256, 128], P('gy', 'gz'), may hold values 0 or 1
- start: float32 [64, 256, 128], P('gy', 'gz'), may hold values from 0 to 1
- cotangent: float32 [64, 256, 128], P('gy', 'gz'), may hold values from -12 to 12
Outputs:
- probability: float32 [64, 256, 128], P('gy', 'gz')
- adjoint: float32 [64, 256, 128], P('gy', 'gz')
- grad_conduct: float32 [64, 256, 128], P('gy', 'gz')
All inputs are finite; a program needn't handle non-finite values. No bound on the sum of `seeds` or of `labels` on one device may be relied on, other than what follows from the above.
Results may differ from a plain program's by a relative error of at most 0.0001.
Values sent between devices are 32-bit elements; how exact they have to be, the bound alone decides.
A program may use at most 64 MiB of HBM per device.

v0:
```python
import jax
import jax.numpy as jnp
from jax import lax
from jax.sharding import PartitionSpec as P

ITERS = 2
seed_pull = 4.0
screening = 0.05


def with_halo(block, sides, width):
    for axis, dim in sides:
        count = lax.axis_size(axis)
        forward = [(i, i + 1) for i in range(count - 1)]
        backward = [(target, source) for source, target in forward]
        low = lax.ppermute(
            lax.slice_in_dim(block, block.shape[dim] - width, None, axis=dim), axis, forward
        )
        high = lax.ppermute(lax.slice_in_dim(block, 0, width, axis=dim), axis, backward)
        block = jnp.concatenate([low, block, high], axis=dim)
    return block


def harmonic(first, second):
    return 2.0 * first * second / (first + second)


def faces(field):
    return with_halo(field, (("gy", 0), ("gz", 1)), 1)


def coefficients(padded_cond, seeds):
    core = padded_cond[1:-1, 1:-1]
    along = jnp.pad(core, ((0, 0), (0, 0), (1, 1)))
    weights = (
        harmonic(core, padded_cond[2:, 1:-1]),
        harmonic(core, padded_cond[:-2, 1:-1]),
        harmonic(core, padded_cond[1:-1, 2:]),
        harmonic(core, padded_cond[1:-1, :-2]),
        harmonic(core, along[..., 2:]),
        harmonic(core, along[..., :-2]),
    )
    diagonal = weights[0] + weights[1] + weights[2] + weights[3] + weights[4] + weights[5]
    diagonal = diagonal + seed_pull * seeds.astype(jnp.float32) + screening
    return (diagonal,) + weights


def operate(padded, coeffs):
    field = padded[1:-1, 1:-1]
    along = jnp.pad(field, ((0, 0), (0, 0), (1, 1)))
    out = coeffs[0] * field - coeffs[1] * padded[2:, 1:-1] - coeffs[2] * padded[:-2, 1:-1]
    out = out - coeffs[3] * padded[1:-1, 2:] - coeffs[4] * padded[1:-1, :-2]
    return out - coeffs[5] * along[..., 2:] - coeffs[6] * along[..., :-2]


def edge_term(ci, cj, ui, uj, vi, vj):
    total = ci + cj
    return -2.0 * cj * cj / (total * total) * (ui - uj) * (vi - vj)


def gradient(cond_pad, prob_pad, adj_pad):
    ci = cond_pad[1:-1, 1:-1]
    ui = prob_pad[1:-1, 1:-1]
    vi = adj_pad[1:-1, 1:-1]
    out = edge_term(ci, cond_pad[2:, 1:-1], ui, prob_pad[2:, 1:-1], vi, adj_pad[2:, 1:-1])
    out = out + edge_term(ci, cond_pad[:-2, 1:-1], ui, prob_pad[:-2, 1:-1], vi, adj_pad[:-2, 1:-1])
    out = out + edge_term(ci, cond_pad[1:-1, 2:], ui, prob_pad[1:-1, 2:], vi, adj_pad[1:-1, 2:])
    out = out + edge_term(ci, cond_pad[1:-1, :-2], ui, prob_pad[1:-1, :-2], vi, adj_pad[1:-1, :-2])
    cx = jnp.pad(ci, ((0, 0), (0, 0), (1, 1)))
    ux = jnp.pad(ui, ((0, 0), (0, 0), (1, 1)))
    vx = jnp.pad(vi, ((0, 0), (0, 0), (1, 1)))
    out = out + edge_term(ci, cx[..., 2:], ui, ux[..., 2:], vi, vx[..., 2:])
    return out + edge_term(ci, cx[..., :-2], ui, ux[..., :-2], vi, vx[..., :-2])


def paired_sums(resid, image):
    return lax.psum((jnp.sum(resid * resid), jnp.sum(resid * image)), ("gy", "gz"))


def conjugate(iterate, iterate_pad, resid, coeffs):
    resid_pad = faces(resid)
    image = operate(resid_pad, coeffs)
    norm_now, product = paired_sums(resid, image)
    alpha = norm_now / product
    direction, direction_pad, along = (resid, resid_pad, image)
    for step in range(ITERS):
        iterate = iterate + alpha * direction
        resid = resid - alpha * along
        if step + 1 < ITERS:
            resid_pad = faces(resid)
            image = operate(resid_pad, coeffs)
            norm_next, product = paired_sums(resid, image)
            ratio = norm_next / norm_now
            alpha = norm_next / (product - ratio * norm_next / alpha)
            direction = resid + ratio * direction
            along = image + ratio * along
            norm_now = norm_next
    return (iterate, iterate_pad)


def per_device(conduct, seeds, labels, start, cotangent):
    cond_pad = with_halo(conduct, (("gy", 0), ("gz", 1)), 1)
    start_pad = faces(start)
    coeffs = coefficients(cond_pad, seeds)
    rhs = seed_pull * (seeds * labels).astype(jnp.float32)
    first_resid = rhs - operate(start_pad, coeffs)
    probability, prob_pad = conjugate(start, start_pad, first_resid, coeffs)
    adjoint, adj_pad = conjugate(
        jnp.zeros_like(cotangent), jnp.zeros_like(start_pad), cotangent, coeffs
    )
    paired = with_halo(jnp.stack([probability, adjoint]), (("gy", 1), ("gz", 2)), 1)
    prob_pad = paired[0]
    adj_pad = paired[1]
    grad_conduct = gradient(cond_pad, prob_pad, adj_pad)
    return (probability, adjoint, grad_conduct)


def solution(mesh):
    in_specs = (
        P("gy", "gz", None),
        P("gy", "gz", None),
        P("gy", "gz", None),
        P("gy", "gz", None),
        P("gy", "gz", None),
    )
    out_specs = (P("gy", "gz", None), P("gy", "gz", None), P("gy", "gz", None))
    return jax.shard_map(
        per_device, mesh=mesh, in_specs=in_specs, out_specs=out_specs, check_vma=False
    )
```

profile of v0, /device:TPU:3, one launch (start us, length us, event | category | flops | bytes accessed | tf_op | source)
XLA Modules:
  0.0 203.1 jit_solution(3476084306509242845)
XLA Ops:
  0.6 0.7 fusion.110
  1.4 1.9 collective-permute-start.4
  3.3 4.3 %collective-permute-start.5 = (f32[1,32,128]{2,1,0:T(8,128)S(1)}, f32[1,32,128]{2,1,0:T(8,128)S(1)}, u32[]{:S(2)}, u32[]{:S(2)}) collective-permute-start(f32[1,32,128]{2,1,0:T(8,128)S(1)} %get-tuple-element.50), channel_id=1, source_target_pairs={{0,8},{8,16},{16,24},{1,9},{9,17},{17,25},{2,10},{10,18},{18,26},{... | collective-permute-start | bytes 49160 | tf_op jit(solution)/shard_map/ppermute | solution.py:16
  7.6 0.7 fusion.111
  8.3 2.2 %collective-permute-start.1 = (f32[1,32,128]{2,1,0:T(8,128)S(1)}, f32[1,32,128]{2,1,0:T(8,128)S(1)}, u32[]{:S(2)}, u32[]{:S(2)}) collective-permute-start(f32[1,32,128]{2,1,0:T(8,128)S(1)} %get-tuple-element.52), channel_id=1, source_target_pairs={{0,8},{8,16},{16,24},{1,9},{9,17},{17,25},{2,10},{10,18},{18,26},{... | collective-permute-start | bytes 49160 | tf_op jit(solution)/shard_map/ppermute | solution.py:16
  10.5 0.7 fusion.112
  11.2 3.0 %collective-permute-start.16 = (f32[1,32,128]{2,1,0:T(8,128)S(1)}, f32[1,32,128]{2,1,0:T(8,128)S(1)}, u32[]{:S(2)}, u32[]{:S(2)}) collective-permute-start(f32[1,32,128]{2,1,0:T(8,128)S(1)} %get-tuple-element.53), channel_id=1, source_target_pairs={{8,0},{16,8},{24,16},{9,1},{17,9},{25,17},{10,2},{18,10},{26,18},{... | collective-permute-start | bytes 49160 | tf_op jit(solution)/shard_map/ppermute | solution.py:19
  14.3 3.1 %collective-permute-start.17 = (f32[1,32,128]{2,1,0:T(8,128)S(1)}, f32[1,32,128]{2,1,0:T(8,128)S(1)}, u32[]{:S(2)}, u32[]{:S(2)}) collective-permute-start(f32[1,32,128]{2,1,0:T(8,128)S(1)} %get-tuple-element.54), channel_id=1, source_target_pairs={{0,8},{8,16},{16,24},{1,9},{9,17},{17,25},{2,10},{10,18},{18,26},{... | collective-permute-start | bytes 49160 | tf_op jit(solution)/shard_map/ppermute | solution.py:16
  17.4 0.0 collective-permute-done.1
  17.4 2.2 %collective-permute-start = (f32[1,32,128]{2,1,0:T(8,128)S(1)}, f32[1,32,128]{2,1,0:T(8,128)S(1)}, u32[]{:S(2)}, u32[]{:S(2)}) collective-permute-start(f32[1,32,128]{2,1,0:T(8,128)S(1)} %get-tuple-element.51), channel_id=1, source_target_pairs={{8,0},{16,8},{24,16},{9,1},{17,9},{25,17},{10,2},{18,10},{26,18},{... | collective-permute-start | bytes 49160 | tf_op jit(solution)/shard_map/ppermute | solution.py:19
  19.6 0.0 copy-start.2
  19.6 1.0 constant_dynamic-update-slice_fusion.1
  20.7 2.2 %collective-permute-done = f32[1,32,128]{2,1,0:T(8,128)S(1)} collective-permute-done((f32[1,32,128]{2,1,0:T(8,128)S(1)}, f32[1,32,128]{2,1,0:T(8,128)S(1)}, u32[]{:S(2)}, u32[]{:S(2)}) %collective-permute-start) | collective-permute-done | bytes 16416 | tf_op jit(solution)/shard_map/ppermute | solution.py:19
  22.8 6.3 %collective-permute-start.3 = (f32[18,1,128]{2,1,0:T(1,128)S(1)}, f32[18,1,128]{2,1,0:T(1,128)S(1)}, u32[]{:S(2)}, u32[]{:S(2)}) collective-permute-start(f32[18,1,128]{2,1,0:T(1,128)S(1)} %get-tuple-element.39), channel_id=1, source_target_pairs={{0,1},{1,2},{2,3},{3,4},{4,5},{5,6},{6,7},{8,9},{9,10},{10,11},{11... | collective-permute-start | bytes 27656 | tf_op jit(solution)/shard_map/ppermute | solution.py:16
  29.2 0.0 collective-permute-done.17
  29.2 1.9 collective-permute-start.2
  31.1 0.0 copy-start.5
  31.2 0.0 collective-permute-done.16
  31.2 1.9 collective-permute-start.18
  33.2 3.6 %collective-permute-start.19 = (f32[18,1,128]{2,1,0:T(1,128)S(1)}, f32[18,1,128]{2,1,0:T(1,128)S(1)}, u32[]{:S(2)}, u32[]{:S(2)}) collective-permute-start(f32[18,1,128]{2,1,0:T(1,128)S(1)} %get-tuple-element.42), channel_id=1, source_target_pairs={{0,1},{1,2},{2,3},{3,4},{4,5},{5,6},{6,7},{8,9},{9,10},{10,11},{11... | collective-permute-start | bytes 27656 | tf_op jit(solution)/shard_map/ppermute | solution.py:16
  36.8 0.0 copy-start
  36.8 0.0 copy-start.1
  36.9 2.1 %collective-permute-start.6 = (f32[18,1,128]{2,1,0:T(1,128)S(1)}, f32[18,1,128]{2,1,0:T(1,128)S(1)}, u32[]{:S(2)}, u32[]{:S(2)}) collective-permute-start(f32[18,1,128]{2,1,0:T(1,128)S(1)} %get-tuple-element.37), channel_id=1, source_target_pairs={{1,0},{2,1},{3,2},{4,3},{5,4},{6,5},{7,6},{9,8},{10,9},{11,10},{12... | collective-permute-start | bytes 27656 | tf_op jit(solution)/shard_map/ppermute | solution.py:19
  39.0 0.0 copy-start.6
  39.0 3.8 %collective-permute-start.7 = (f32[18,1,128]{2,1,0:T(1,128)S(1)}, f32[18,1,128]{2,1,0:T(1,128)S(1)}, u32[]{:S(2)}, u32[]{:S(2)}) collective-permute-start(f32[18,1,128]{2,1,0:T(1,128)S(1)} %get-tuple-element.38), channel_id=1, source_target_pairs={{0,1},{1,2},{2,3},{3,4},{4,5},{5,6},{6,7},{8,9},{9,10},{10,11},{11... | collective-permute-start | bytes 27656 | tf_op jit(solution)/shard_map/ppermute | solution.py:16
  42.8 0.0 collective-permute-done.2
  42.8 0.0 collective-permute-done.19
  42.8 1.2 multiply_reduce_fusion.1
  44.1 0.0 collective-permute-done.6
  44.1 0.4 fusion.26
  44.5 1.9 collective-permute-start.9
  46.4 3.4 %collective-permute-start.8 = (f32[1,32,128]{2,1,0:T(8,128)S(1)}, f32[1,32,128]{2,1,0:T(8,128)S(1)}, u32[]{:S(2)}, u32[]{:S(2)}) collective-permute-start(f32[1,32,128]{2,1,0:T(8,128)S(1)} %get-tuple-element.48), channel_id=1, source_target_pairs={{8,0},{16,8},{24,16},{9,1},{17,9},{25,17},{10,2},{18,10},{26,18},{... | collective-permute-start | bytes 49160 | tf_op jit(solution)/shard_map/ppermute | solution.py:19
  49.8 2.0 collective-permute-done.8
  51.8 1.9 collective-permute-start.10
  53.8 4.8 %collective-permute-start.11 = (f32[18,1,128]{2,1,0:T(1,128)S(1)}, f32[18,1,128]{2,1,0:T(1,128)S(1)}, u32[]{:S(2)}, u32[]{:S(2)}) collective-permute-start(f32[18,1,128]{2,1,0:T(1,128)S(1)} %get-tuple-element.36), channel_id=1, source_target_pairs={{0,1},{1,2},{2,3},{3,4},{4,5},{5,6},{6,7},{8,9},{9,10},{10,11},{11... | collective-permute-start | bytes 27656 | tf_op jit(solution)/shard_map/ppermute | solution.py:16
  58.6 0.8 collective-permute-done.11
  59.4 1.0 multiply_reduce_fusion.4
  60.4 40.6 %all-reduce.9 = (f32[]{:T(128)}, f32[]{:T(128)}, f32[]{:T(128)}, f32[]{:T(128)}) all-reduce(f32[]{:T(128)} %get-tuple-element.6, f32[]{:T(128)} %get-tuple-element.5, f32[]{:T(128)} %get-tuple-element.4, f32[]{:T(128)} %get-tuple-element.3), channel_id=1, replica_groups=mesh['gy'=4,'gz'=8] {'gy','gz'}, use_global_device_ids=true, to_apply=%region_1.2 | all-reduce | flops 4 | bytes 32 | tf_op jit(solution)/shard_map/psum | solution.py:77
  102.3 0.7 multiply_reduce_fusion
  103.0 0.6 fusion.107
  103.6 3.1 %collective-permute-start.21 = (f32[1,32,128]{2,1,0:T(8,128)}, f32[1,32,128]{2,1,0:T(8,128)S(1)}, u32[]{:S(2)}, u32[]{:S(2)}) collective-permute-start(f32[1,32,128]{2,1,0:T(8,128)} %get-tuple-element.43), channel_id=1, source_target_pairs={{0,8},{8,16},{16,24},{1,9},{9,17},{17,25},{2,10},{10,18},{18,26},{... | collective-permute-start | bytes 49160 | tf_op jit(solution)/shard_map/ppermute | solution.py:16
  106.7 2.2 %collective-permute-start.20 = (f32[1,32,128]{2,1,0:T(8,128)S(1)}, f32[1,32,128]{2,1,0:T(8,128)S(1)}, u32[]{:S(2)}, u32[]{:S(2)}) collective-permute-start(f32[1,32,128]{2,1,0:T(8,128)S(1)} %get-tuple-element.44), channel_id=1, source_target_pairs={{8,0},{16,8},{24,16},{9,1},{17,9},{25,17},{10,2},{18,10},{26,18},{... | collective-permute-start | bytes 49160 | tf_op jit(solution)/shard_map/ppermute | solution.py:19
  110.3 0.7 multiply_reduce_fusion.3
  111.0 4.0 %collective-permute-start.13 = (f32[1,32,128]{2,1,0:T(8,128)S(1)}, f32[1,32,128]{2,1,0:T(8,128)S(1)}, u32[]{:S(2)}, u32[]{:S(2)}) collective-permute-start(f32[1,32,128]{2,1,0:T(8,128)S(1)} %get-tuple-element.45), channel_id=1, source_target_pairs={{0,8},{8,16},{16,24},{1,9},{9,17},{17,25},{2,10},{10,18},{18,26},{... | collective-permute-start | bytes 49160 | tf_op jit(solution)/shard_map/ppermute | solution.py:16
  115.0 1.9 collective-permute-start.12
  116.9 4.8 %collective-permute-start.22 = (f32[18,1,128]{2,1,0:T(1,128)S(1)}, f32[18,1,128]{2,1,0:T(1,128)S(1)}, u32[]{:S(2)}, u32[]{:S(2)}) collective-permute-start(f32[18,1,128]{2,1,0:T(1,128)S(1)} %get-tuple-element.31), channel_id=1, source_target_pairs={{1,0},{2,1},{3,2},{4,3},{5,4},{6,5},{7,6},{9,8},{10,9},{11,10},{12... | collective-permute-start | bytes 27656 | tf_op jit(solution)/shard_map/ppermute | solution.py:19
  121.7 3.0 %collective-permute-start.23 = (f32[18,1,128]{2,1,0:T(1,128)S(1)}, f32[18,1,128]{2,1,0:T(1,128)S(1)}, u32[]{:S(2)}, u32[]{:S(2)}) collective-permute-start(f32[18,1,128]{2,1,0:T(1,128)S(1)} %get-tuple-element.32), channel_id=1, source_target_pairs={{0,1},{1,2},{2,3},{3,4},{4,5},{5,6},{6,7},{8,9},{9,10},{10,11},{11... | collective-permute-start | bytes 27656 | tf_op jit(solution)/shard_map/ppermute | solution.py:16
  124.8 1.9 collective-permute-start.14
  126.7 3.6 %collective-permute-start.15 = (f32[18,1,128]{2,1,0:T(1,128)S(1)}, f32[18,1,128]{2,1,0:T(1,128)S(1)}, u32[]{:S(2)}, u32[]{:S(2)}) collective-permute-start(f32[18,1,128]{2,1,0:T(1,128)S(1)} %get-tuple-element.34), channel_id=1, source_target_pairs={{0,1},{1,2},{2,3},{3,4},{4,5},{5,6},{6,7},{8,9},{9,10},{10,11},{11... | collective-permute-start | bytes 27656 | tf_op jit(solution)/shard_map/ppermute | solution.py:16
  130.4 1.0 fusion.46
  131.4 1.0 fusion.36
  132.4 41.4 %all-reduce.8 = (f32[]{:T(128)}, f32[]{:T(128)}, f32[]{:T(128)}, f32[]{:T(128)}) all-reduce(f32[]{:T(128)} %get-tuple-element.17, f32[]{:T(128)} %fusion.36, f32[]{:T(128)} %get-tuple-element.15, f32[]{:T(128)} %fusion.46), channel_id=1, replica_groups=mesh['gy'=4,'gz'=8] {'gy','gz'}, use_global_device_ids=true, to_apply=%region_5.6 | all-reduce | flops 4 | bytes 32 | tf_op jit(solution)/shard_map/psum | solution.py:77
  183.1 0.1 multiply_add_fusion
  183.2 0.0 copy-start.3
  183.2 0.0 copy-start.4
  183.2 3.1 %collective-permute-start.24 = (f32[2,1,32,128]{3,2,1,0:T(8,128)S(1)}, f32[2,1,32,128]{3,2,1,0:T(8,128)S(1)}, u32[]{:S(2)}, u32[]{:S(2)}) collective-permute-start(f32[2,1,32,128]{3,2,1,0:T(8,128)S(1)} %get-tuple-element.29), channel_id=1, source_target_pairs={{0,8},{8,16},{16,24},{1,9},{9,17},{17,25},{2,10},{10,18},{18,26},{... | collective-permute-start | bytes 98312 | tf_op jit(solution)/shard_map/ppermute | solution.py:16
  186.4 2.2 %collective-permute-start.25 = (f32[2,1,32,128]{3,2,1,0:T(8,128)S(1)}, f32[2,1,32,128]{3,2,1,0:T(8,128)S(1)}, u32[]{:S(2)}, u32[]{:S(2)}) collective-permute-start(f32[2,1,32,128]{3,2,1,0:T(8,128)S(1)} %get-tuple-element.30), channel_id=1, source_target_pairs={{8,0},{16,8},{24,16},{9,1},{17,9},{25,17},{10,2},{18,10},{26,18},{... | collective-permute-start | bytes 98312 | tf_op jit(solution)/shard_map/ppermute | solution.py:19
  188.6 3.4 %collective-permute-done.25 = f32[2,1,32,128]{3,2,1,0:T(8,128)S(1)} collective-permute-done((f32[2,1,32,128]{3,2,1,0:T(8,128)S(1)}, f32[2,1,32,128]{3,2,1,0:T(8,128)S(1)}, u32[]{:S(2)}, u32[]{:S(2)}) %collective-permute-start.25) | collective-permute-done | bytes 32800 | tf_op jit(solution)/shard_map/ppermute | solution.py:19
  191.9 4.4 %collective-permute-start.26 = (f32[2,18,1,128]{3,2,1,0:T(1,128)S(1)}, f32[2,18,1,128]{3,2,1,0:T(1,128)S(1)}, u32[]{:S(2)}, u32[]{:S(2)}) collective-permute-start(f32[2,18,1,128]{3,2,1,0:T(1,128)S(1)} %get-tuple-element.27), channel_id=1, source_target_pairs={{0,1},{1,2},{2,3},{3,4},{4,5},{5,6},{6,7},{8,9},{9,10},{10,11},{11... | collective-permute-start | bytes 55304 | tf_op jit(solution)/shard_map/ppermute | solution.py:16
  196.4 1.9 collective-permute-start.27
  198.3 3.1 %collective-permute-done.27 = f32[2,18,1,128]{3,2,1,0:T(1,128)S(1)} collective-permute-done((f32[2,18,1,128]{3,2,1,0:T(1,128)S(1)}, f32[2,18,1,128]{3,2,1,0:T(1,128)S(1)}, u32[]{:S(2)}, u32[]{:S(2)}) %collective-permute-start.27) | collective-permute-done | bytes 18464 | tf_op jit(solution)/shard_map/ppermute | solution.py:19
  201.4 0.1 pad_maximum_fusion
  201.5 0.1 slice_bitcast_fusion
  201.7 1.4 fusion.7
  (44 shorter events, 0.3 us)
Async XLA Ops:
  1.4 35.5 %collective-permute-start.4 = (f32[1,32,128]{2,1,0:T(8,128)S(1)}, f32[1,32,128]{2,1,0:T(8,128)S(1)}, u32[]{:S(2)}, u32[]{:S(2)}) collective-permute-start(f32[1,32,128]{2,1,0:T(8,128)S(1)} %get-tuple-element.49), channel_id=1, source_target_pairs={{8,0},{16,8},{24,16},{9,1},{17,9},{25,17},{10,2},{18,10},{26,18},{... | collective-permute-start | bytes 49160 | tf_op jit(solution)/shard_map/ppermute | solution.py:19
  3.3 29.9 %collective-permute-start.5 = (f32[1,32,128]{2,1,0:T(8,128)S(1)}, f32[1,32,128]{2,1,0:T(8,128)S(1)}, u32[]{:S(2)}, u32[]{:S(2)}) collective-permute-start(f32[1,32,128]{2,1,0:T(8,128)S(1)} %get-tuple-element.50), channel_id=1, source_target_pairs={{0,8},{8,16},{16,24},{1,9},{9,17},{17,25},{2,10},{10,18},{18,26},{... | collective-permute-start | bytes 49160 | tf_op jit(solution)/shard_map/ppermute | solution.py:16
  8.3 9.1 %collective-permute-start.1 = (f32[1,32,128]{2,1,0:T(8,128)S(1)}, f32[1,32,128]{2,1,0:T(8,128)S(1)}, u32[]{:S(2)}, u32[]{:S(2)}) collective-permute-start(f32[1,32,128]{2,1,0:T(8,128)S(1)} %get-tuple-element.52), channel_id=1, source_target_pairs={{0,8},{8,16},{16,24},{1,9},{9,17},{17,25},{2,10},{10,18},{18,26},{... | collective-permute-start | bytes 49160 | tf_op jit(solution)/shard_map/ppermute | solution.py:16
  11.2 19.9 %collective-permute-start.16 = (f32[1,32,128]{2,1,0:T(8,128)S(1)}, f32[1,32,128]{2,1,0:T(8,128)S(1)}, u32[]{:S(2)}, u32[]{:S(2)}) collective-permute-start(f32[1,32,128]{2,1,0:T(8,128)S(1)} %get-tuple-element.53), channel_id=1, source_target_pairs={{8,0},{16,8},{24,16},{9,1},{17,9},{25,17},{10,2},{18,10},{26,18},{... | collective-permute-start | bytes 49160 | tf_op jit(solution)/shard_map/ppermute | solution.py:19
  14.3 14.9 %collective-permute-start.17 = (f32[1,32,128]{2,1,0:T(8,128)S(1)}, f32[1,32,128]{2,1,0:T(8,128)S(1)}, u32[]{:S(2)}, u32[]{:S(2)}) collective-permute-start(f32[1,32,128]{2,1,0:T(8,128)S(1)} %get-tuple-element.54), channel_id=1, source_target_pairs={{0,8},{8,16},{16,24},{1,9},{9,17},{17,25},{2,10},{10,18},{18,26},{... | collective-permute-start | bytes 49160 | tf_op jit(solution)/shard_map/ppermute | solution.py:16
  17.4 5.4 %collective-permute-start = (f32[1,32,128]{2,1,0:T(8,128)S(1)}, f32[1,32,128]{2,1,0:T(8,128)S(1)}, u32[]{:S(2)}, u32[]{:S(2)}) collective-permute-start(f32[1,32,128]{2,1,0:T(8,128)S(1)} %get-tuple-element.51), channel_id=1, source_target_pairs={{8,0},{16,8},{24,16},{9,1},{17,9},{25,17},{10,2},{18,10},{26,18},{... | collective-permute-start | bytes 49160 | tf_op jit(solution)/shard_map/ppermute | solution.py:19
  19.6 11.5 %copy-start.2 = (f32[16,32,128]{2,1,0:T(8,128)S(1)}, f32[16,32,128]{2,1,0:T(8,128)}, u32[]{:S(2)}) copy-start(f32[16,32,128]{2,1,0:T(8,128)} %param.9) | copy-start | bytes 786436
  22.8 16.1 %collective-permute-start.3 = (f32[18,1,128]{2,1,0:T(1,128)S(1)}, f32[18,1,128]{2,1,0:T(1,128)S(1)}, u32[]{:S(2)}, u32[]{:S(2)}) collective-permute-start(f32[18,1,128]{2,1,0:T(1,128)S(1)} %get-tuple-element.39), channel_id=1, source_target_pairs={{0,1},{1,2},{2,3},{3,4},{4,5},{5,6},{6,7},{8,9},{9,10},{10,11},{11... | collective-permute-start | bytes 27656 | tf_op jit(solution)/shard_map/ppermute | solution.py:16
  29.2 13.6 %collective-permute-start.2 = (f32[18,1,128]{2,1,0:T(1,128)S(1)}, f32[18,1,128]{2,1,0:T(1,128)S(1)}, u32[]{:S(2)}, u32[]{:S(2)}) collective-permute-start(f32[18,1,128]{2,1,0:T(1,128)S(1)} %get-tuple-element.40), channel_id=1, source_target_pairs={{1,0},{2,1},{3,2},{4,3},{5,4},{6,5},{7,6},{9,8},{10,9},{11,10},{12... | collective-permute-start | bytes 27656 | tf_op jit(solution)/shard_map/ppermute | solution.py:19
  31.1 5.7 %copy-start.5 = (f32[16,32,128]{2,1,0:T(8,128)S(1)}, f32[16,32,128]{2,1,0:T(8,128)}, u32[]{:S(2)}) copy-start(f32[16,32,128]{2,1,0:T(8,128)} %param.8) | copy-start | bytes 786436
  31.2 11.6 %collective-permute-start.18 = (f32[18,1,128]{2,1,0:T(1,128)S(1)}, f32[18,1,128]{2,1,0:T(1,128)S(1)}, u32[]{:S(2)}, u32[]{:S(2)}) collective-permute-start(f32[18,1,128]{2,1,0:T(1,128)S(1)} %get-tuple-element.41), channel_id=1, source_target_pairs={{1,0},{2,1},{3,2},{4,3},{5,4},{6,5},{7,6},{9,8},{10,9},{11,10},{12... | collective-permute-start | bytes 27656 | tf_op jit(solution)/shard_map/ppermute | solution.py:19
  33.2 9.7 %collective-permute-start.19 = (f32[18,1,128]{2,1,0:T(1,128)S(1)}, f32[18,1,128]{2,1,0:T(1,128)S(1)}, u32[]{:S(2)}, u32[]{:S(2)}) collective-permute-start(f32[18,1,128]{2,1,0:T(1,128)S(1)} %get-tuple-element.42), channel_id=1, source_target_pairs={{0,1},{1,2},{2,3},{3,4},{4,5},{5,6},{6,7},{8,9},{9,10},{10,11},{11... | collective-permute-start | bytes 27656 | tf_op jit(solution)/shard_map/ppermute | solution.py:16
  36.8 6.0 %copy-start = (f32[16,32,128]{2,1,0:T(8,128)S(1)}, f32[16,32,128]{2,1,0:T(8,128)}, u32[]{:S(2)}) copy-start(f32[16,32,128]{2,1,0:T(8,128)} %param.5) | copy-start | bytes 786436
  36.8 6.0 %copy-start.1 = (s32[16,32,128]{2,1,0:T(8,128)S(1)}, s32[16,32,128]{2,1,0:T(8,128)}, u32[]{:S(2)}) copy-start(s32[16,32,128]{2,1,0:T(8,128)} %param.6) | copy-start | bytes 786436
  36.9 7.2 %collective-permute-start.6 = (f32[18,1,128]{2,1,0:T(1,128)S(1)}, f32[18,1,128]{2,1,0:T(1,128)S(1)}, u32[]{:S(2)}, u32[]{:S(2)}) collective-permute-start(f32[18,1,128]{2,1,0:T(1,128)S(1)} %get-tuple-element.37), channel_id=1, source_target_pairs={{1,0},{2,1},{3,2},{4,3},{5,4},{6,5},{7,6},{9,8},{10,9},{11,10},{12... | collective-permute-start | bytes 27656 | tf_op jit(solution)/shard_map/ppermute | solution.py:19
  39.0 5.1 %copy-start.6 = (s32[16,32,128]{2,1,0:T(8,128)S(1)}, s32[16,32,128]{2,1,0:T(8,128)}, u32[]{:S(2)}) copy-start(s32[16,32,128]{2,1,0:T(8,128)} %param.7) | copy-start | bytes 786436
  39.0 5.1 %collective-permute-start.7 = (f32[18,1,128]{2,1,0:T(1,128)S(1)}, f32[18,1,128]{2,1,0:T(1,128)S(1)}, u32[]{:S(2)}, u32[]{:S(2)}) collective-permute-start(f32[18,1,128]{2,1,0:T(1,128)S(1)} %get-tuple-element.38), channel_id=1, source_target_pairs={{0,1},{1,2},{2,3},{3,4},{4,5},{5,6},{6,7},{8,9},{9,10},{10,11},{11... | collective-permute-start | bytes 27656 | tf_op jit(solution)/shard_map/ppermute | solution.py:16
  44.5 5.3 %collective-permute-start.9 = (f32[1,32,128]{2,1,0:T(8,128)S(1)}, f32[1,32,128]{2,1,0:T(8,128)S(1)}, u32[]{:S(2)}, u32[]{:S(2)}) collective-permute-start(f32[1,32,128]{2,1,0:T(8,128)S(1)} %get-tuple-element.47), channel_id=1, source_target_pairs={{0,8},{8,16},{16,24},{1,9},{9,17},{17,25},{2,10},{10,18},{18,26},{... | collective-permute-start | bytes 49160 | tf_op jit(solution)/shard_map/ppermute | solution.py:16
  46.4 5.4 %collective-permute-start.8 = (f32[1,32,128]{2,1,0:T(8,128)S(1)}, f32[1,32,128]{2,1,0:T(8,128)S(1)}, u32[]{:S(2)}, u32[]{:S(2)}) collective-permute-start(f32[1,32,128]{2,1,0:T(8,128)S(1)} %get-tuple-element.48), channel_id=1, source_target_pairs={{8,0},{16,8},{24,16},{9,1},{17,9},{25,17},{10,2},{18,10},{26,18},{... | collective-permute-start | bytes 49160 | tf_op jit(solution)/shard_map/ppermute | solution.py:19
  51.8 6.8 %collective-permute-start.10 = (f32[18,1,128]{2,1,0:T(1,128)S(1)}, f32[18,1,128]{2,1,0:T(1,128)S(1)}, u32[]{:S(2)}, u32[]{:S(2)}) collective-permute-start(f32[18,1,128]{2,1,0:T(1,128)S(1)} %get-tuple-element.35), channel_id=1, source_target_pairs={{1,0},{2,1},{3,2},{4,3},{5,4},{6,5},{7,6},{9,8},{10,9},{11,10},{12... | collective-permute-start | bytes 27656 | tf_op jit(solution)/shard_map/ppermute | solution.py:19
  53.8 5.6 %collective-permute-start.11 = (f32[18,1,128]{2,1,0:T(1,128)S(1)}, f32[18,1,128]{2,1,0:T(1,128)S(1)}, u32[]{:S(2)}, u32[]{:S(2)}) collective-permute-start(f32[18,1,128]{2,1,0:T(1,128)S(1)} %get-tuple-element.36), channel_id=1, source_target_pairs={{0,1},{1,2},{2,3},{3,4},{4,5},{5,6},{6,7},{8,9},{9,10},{10,11},{11... | collective-permute-start | bytes 27656 | tf_op jit(solution)/shard_map/ppermute | solution.py:16
  103.6 13.3 %collective-permute-start.21 = (f32[1,32,128]{2,1,0:T(8,128)}, f32[1,32,128]{2,1,0:T(8,128)S(1)}, u32[]{:S(2)}, u32[]{:S(2)}) collective-permute-start(f32[1,32,128]{2,1,0:T(8,128)} %get-tuple-element.43), channel_id=1, source_target_pairs={{0,8},{8,16},{16,24},{1,9},{9,17},{17,25},{2,10},{10,18},{18,26},{... | collective-permute-start | bytes 49160 | tf_op jit(solution)/shard_map/ppermute | solution.py:16
  106.7 10.2 %collective-permute-start.20 = (f32[1,32,128]{2,1,0:T(8,128)S(1)}, f32[1,32,128]{2,1,0:T(8,128)S(1)}, u32[]{:S(2)}, u32[]{:S(2)}) collective-permute-start(f32[1,32,128]{2,1,0:T(8,128)S(1)} %get-tuple-element.44), channel_id=1, source_target_pairs={{8,0},{16,8},{24,16},{9,1},{17,9},{25,17},{10,2},{18,10},{26,18},{... | collective-permute-start | bytes 49160 | tf_op jit(solution)/shard_map/ppermute | solution.py:19
  111.0 13.8 %collective-permute-start.13 = (f32[1,32,128]{2,1,0:T(8,128)S(1)}, f32[1,32,128]{2,1,0:T(8,128)S(1)}, u32[]{:S(2)}, u32[]{:S(2)}) collective-permute-start(f32[1,32,128]{2,1,0:T(8,128)S(1)} %get-tuple-element.45), channel_id=1, source_target_pairs={{0,8},{8,16},{16,24},{1,9},{9,17},{17,25},{2,10},{10,18},{18,26},{... | collective-permute-start | bytes 49160 | tf_op jit(solution)/shard_map/ppermute | solution.py:16
  115.0 9.8 %collective-permute-start.12 = (f32[1,32,128]{2,1,0:T(8,128)S(1)}, f32[1,32,128]{2,1,0:T(8,128)S(1)}, u32[]{:S(2)}, u32[]{:S(2)}) collective-permute-start(f32[1,32,128]{2,1,0:T(8,128)S(1)} %get-tuple-element.46), channel_id=1, source_target_pairs={{8,0},{16,8},{24,16},{9,1},{17,9},{25,17},{10,2},{18,10},{26,18},{... | collective-permute-start | bytes 49160 | tf_op jit(solution)/shard_map/ppermute | solution.py:19
  116.9 13.4 %collective-permute-start.22 = (f32[18,1,128]{2,1,0:T(1,128)S(1)}, f32[18,1,128]{2,1,0:T(1,128)S(1)}, u32[]{:S(2)}, u32[]{:S(2)}) collective-permute-start(f32[18,1,128]{2,1,0:T(1,128)S(1)} %get-tuple-element.31), channel_id=1, source_target_pairs={{1,0},{2,1},{3,2},{4,3},{5,4},{6,5},{7,6},{9,8},{10,9},{11,10},{12... | collective-permute-start | bytes 27656 | tf_op jit(solution)/shard_map/ppermute | solution.py:19
  121.7 8.7 %collective-permute-start.23 = (f32[18,1,128]{2,1,0:T(1,128)S(1)}, f32[18,1,128]{2,1,0:T(1,128)S(1)}, u32[]{:S(2)}, u32[]{:S(2)}) collective-permute-start(f32[18,1,128]{2,1,0:T(1,128)S(1)} %get-tuple-element.32), channel_id=1, source_target_pairs={{0,1},{1,2},{2,3},{3,4},{4,5},{5,6},{6,7},{8,9},{9,10},{10,11},{11... | collective-permute-start | bytes 27656 | tf_op jit(solution)/shard_map/ppermute | solution.py:16
  124.8 6.6 %collective-permute-start.14 = (f32[18,1,128]{2,1,0:T(1,128)S(1)}, f32[18,1,128]{2,1,0:T(1,128)S(1)}, u32[]{:S(2)}, u32[]{:S(2)}) collective-permute-start(f32[18,1,128]{2,1,0:T(1,128)S(1)} %get-tuple-element.33), channel_id=1, source_target_pairs={{1,0},{2,1},{3,2},{4,3},{5,4},{6,5},{7,6},{9,8},{10,9},{11,10},{12... | collective-permute-start | bytes 27656 | tf_op jit(solution)/shard_map/ppermute | solution.py:19
  126.7 4.7 %collective-permute-start.15 = (f32[18,1,128]{2,1,0:T(1,128)S(1)}, f32[18,1,128]{2,1,0:T(1,128)S(1)}, u32[]{:S(2)}, u32[]{:S(2)}) collective-permute-start(f32[18,1,128]{2,1,0:T(1,128)S(1)} %get-tuple-element.34), channel_id=1, source_target_pairs={{0,1},{1,2},{2,3},{3,4},{4,5},{5,6},{6,7},{8,9},{9,10},{10,11},{11... | collective-permute-start | bytes 27656 | tf_op jit(solution)/shard_map/ppermute | solution.py:16
  183.2 18.2 %copy-start.3 = (f32[16,32,128]{2,1,0:T(8,128)}, f32[16,32,128]{2,1,0:T(8,128)S(1)}, u32[]{:S(2)}) copy-start(f32[16,32,128]{2,1,0:T(8,128)S(1)} %get-tuple-element.55) | copy-start | bytes 786436
  183.2 18.2 %copy-start.4 = (f32[16,32,128]{2,1,0:T(8,128)}, f32[16,32,128]{2,1,0:T(8,128)S(1)}, u32[]{:S(2)}) copy-start(f32[16,32,128]{2,1,0:T(8,128)S(1)} %get-tuple-element.56) | copy-start | bytes 786436
  183.2 5.3 %collective-permute-start.24 = (f32[2,1,32,128]{3,2,1,0:T(8,128)S(1)}, f32[2,1,32,128]{3,2,1,0:T(8,128)S(1)}, u32[]{:S(2)}, u32[]{:S(2)}) collective-permute-start(f32[2,1,32,128]{3,2,1,0:T(8,128)S(1)} %get-tuple-element.29), channel_id=1, source_target_pairs={{0,8},{8,16},{16,24},{1,9},{9,17},{17,25},{2,10},{10,18},{18,26},{... | collective-permute-start | bytes 98312 | tf_op jit(solution)/shard_map/ppermute | solution.py:16
  186.4 5.6 %collective-permute-start.25 = (f32[2,1,32,128]{3,2,1,0:T(8,128)S(1)}, f32[2,1,32,128]{3,2,1,0:T(8,128)S(1)}, u32[]{:S(2)}, u32[]{:S(2)}) collective-permute-start(f32[2,1,32,128]{3,2,1,0:T(8,128)S(1)} %get-tuple-element.30), channel_id=1, source_target_pairs={{8,0},{16,8},{24,16},{9,1},{17,9},{25,17},{10,2},{18,10},{26,18},{... | collective-permute-start | bytes 98312 | tf_op jit(solution)/shard_map/ppermute | solution.py:19
  191.9 6.3 %collective-permute-start.26 = (f32[2,18,1,128]{3,2,1,0:T(1,128)S(1)}, f32[2,18,1,128]{3,2,1,0:T(1,128)S(1)}, u32[]{:S(2)}, u32[]{:S(2)}) collective-permute-start(f32[2,18,1,128]{3,2,1,0:T(1,128)S(1)} %get-tuple-element.27), channel_id=1, source_target_pairs={{0,1},{1,2},{2,3},{3,4},{4,5},{5,6},{6,7},{8,9},{9,10},{10,11},{11... | collective-permute-start | bytes 55304 | tf_op jit(solution)/shard_map/ppermute | solution.py:16
  196.4 5.1 %collective-permute-start.27 = (f32[2,18,1,128]{3,2,1,0:T(1,128)S(1)}, f32[2,18,1,128]{3,2,1,0:T(1,128)S(1)}, u32[]{:S(2)}, u32[]{:S(2)}) collective-permute-start(f32[2,18,1,128]{3,2,1,0:T(1,128)S(1)} %get-tuple-element.28), channel_id=1, source_target_pairs={{1,0},{2,1},{3,2},{4,3},{5,4},{6,5},{7,6},{9,8},{10,9},{11,10},{12... | collective-permute-start | bytes 55304 | tf_op jit(solution)/shard_map/ppermute | solution.py:19
where the time goes:
time: 205 us; the launch traced here: 203 us
  starting transfers between devices  84.5 us (41%)
  blocking collectives  82 us (40%)
  between operations  13.2 us (6%)
  waiting for transfers between devices  11.5 us (6%)
  other arithmetic  7.82 us (4%)
  local copies, waits for them, and re-layouts  4.1 us (2%)
    psum x2, blocking collectives, paired_sums(): lax.psum((jnp.sum(resid * resid), jnp.sum(resid * image)), ('gy', 'gz'))  82 us
    ppermute x14, starting transfers between devices, with_halo(): lax.ppermute(lax.slice_in_dim(block, block.shape[dim] - width, None, axis...  51.3 us
    ppermute x14, starting transfers between devices, with_halo(): lax.ppermute(lax.slice_in_dim(block, 0, width, axis=dim), axis, backward)  33.2 us
    ppermute x14, waiting for transfers between devices, with_halo(): lax.ppermute(lax.slice_in_dim(block, 0, width, axis=dim), axis, backward)  10.7 us
    reduce_sum x4, other arithmetic, paired_sums(): jnp.sum(resid * image)  4.26 us
  transfers between devices with their start and end apart: 28, of which 5 were waited for; matrix products, arithmetic and copies ran while one was open for 3% of the time, Pallas kernels for 0%

commit v1 on v0

--- a/solution.py
+++ b/solution.py
@@ -74,7 +74,7 @@
 
 
 def paired_sums(resid, image):
-    return lax.psum((jnp.sum(resid * resid), jnp.sum(resid * image)), ("gy", "gz"))
+    return lax.psum(lax.psum((jnp.sum(resid * resid), jnp.sum(resid * image)), "gz"), "gy")
 
 
 def conjugate(iterate, iterate_pad, resid, coeffs):

time: 205 us -> 168 us (0.82)
  blocking collectives: 82 us -> 43.5 us
  starting transfers between devices: 84.5 us -> 87.6 us
    psum x2 -> x4, blocking collectives: 82 us -> 43.5 us  [the longest x2 28 us: paired_sums(): lax.psum((jnp.sum(resid * resid), jnp.sum(resid * image)), 'gz')]
    ppermute x14, starting transfers between devices: 33.2 us -> 37.4 us  [with_halo(): lax.ppermute(lax.slice_in_dim(block, 0, width, axis=dim), axis, backward)]
where the time goes in v1:
time: 168 us; the launch traced here: 166 us
  starting transfers between devices  87.6 us (52%)
  blocking collectives  43.5 us (26%)
  between operations  13.2 us (8%)
  waiting for transfers between devices  10.1 us (6%)
  other arithmetic  7.91 us (5%)
  local copies, waits for them, and re-layouts  4.1 us (2%)
    ppermute x14, starting transfers between devices, with_halo(): lax.ppermute(lax.slice_in_dim(block, block.shape[dim] - width, None, axis...  50.2 us
    ppermute x14, starting transfers between devices, with_halo(): lax.ppermute(lax.slice_in_dim(block, 0, width, axis=dim), axis, backward)  37.4 us
    psum x2, blocking collectives, paired_sums(): lax.psum((jnp.sum(resid * resid), jnp.sum(resid * image)), 'gz')  28 us
    psum x2, blocking collectives, paired_sums(): lax.psum(lax.psum((jnp.sum(resid * resid), jnp.sum(resid * image)), 'gz')...  15.5 us
    ppermute x14, waiting for transfers between devices, with_halo(): lax.ppermute(lax.slice_in_dim(block, 0, width, axis=dim), axis, backward)  9.29 us
    reduce_sum x4, other arithmetic, paired_sums(): jnp.sum(resid * image)  4.26 us
  transfers between devices with their start and end apart: 28, of which 5 were waited for; matrix products, arithmetic and copies ran while one was open for 3% of the time, Pallas kernels for 0%

profile of v1, /device:TPU:3, one launch (start us, length us, event | category | flops | bytes accessed | tf_op | source)
XLA Modules:
  0.0 166.4 jit_solution(7166693965967703496)
XLA Ops:
  0.6 0.7 fusion.110
  1.4 1.9 %collective-permute-start.4 = (f32[1,32,128]{2,1,0:T(8,128)S(1)}, f32[1,32,128]{2,1,0:T(8,128)S(1)}, u32[]{:S(2)}, u32[]{:S(2)}) collective-permute-start(f32[1,32,128]{2,1,0:T(8,128)S(1)} %get-tuple-element.57), channel_id=1, source_target_pairs={{8,0},{16,8},{24,16},{9,1},{17,9},{25,17},{10,2},{18,10},{26,18},{... | collective-permute-start | bytes 49160 | tf_op jit(solution)/shard_map/ppermute | solution.py:19
  3.3 4.3 %collective-permute-start.5 = (f32[1,32,128]{2,1,0:T(8,128)S(1)}, f32[1,32,128]{2,1,0:T(8,128)S(1)}, u32[]{:S(2)}, u32[]{:S(2)}) collective-permute-start(f32[1,32,128]{2,1,0:T(8,128)S(1)} %get-tuple-element.58), channel_id=1, source_target_pairs={{0,8},{8,16},{16,24},{1,9},{9,17},{17,25},{2,10},{10,18},{18,26},{... | collective-permute-start | bytes 49160 | tf_op jit(solution)/shard_map/ppermute | solution.py:16
  7.6 0.7 fusion.111
  8.3 2.2 %collective-permute-start.1 = (f32[1,32,128]{2,1,0:T(8,128)S(1)}, f32[1,32,128]{2,1,0:T(8,128)S(1)}, u32[]{:S(2)}, u32[]{:S(2)}) collective-permute-start(f32[1,32,128]{2,1,0:T(8,128)S(1)} %get-tuple-element.60), channel_id=1, source_target_pairs={{0,8},{8,16},{16,24},{1,9},{9,17},{17,25},{2,10},{10,18},{18,26},{... | collective-permute-start | bytes 49160 | tf_op jit(solution)/shard_map/ppermute | solution.py:16
  10.5 0.7 fusion.112
  11.2 3.0 %collective-permute-start.16 = (f32[1,32,128]{2,1,0:T(8,128)S(1)}, f32[1,32,128]{2,1,0:T(8,128)S(1)}, u32[]{:S(2)}, u32[]{:S(2)}) collective-permute-start(f32[1,32,128]{2,1,0:T(8,128)S(1)} %get-tuple-element.61), channel_id=1, source_target_pairs={{8,0},{16,8},{24,16},{9,1},{17,9},{25,17},{10,2},{18,10},{26,18},{... | collective-permute-start | bytes 49160 | tf_op jit(solution)/shard_map/ppermute | solution.py:19
  14.3 3.1 %collective-permute-start.17 = (f32[1,32,128]{2,1,0:T(8,128)S(1)}, f32[1,32,128]{2,1,0:T(8,128)S(1)}, u32[]{:S(2)}, u32[]{:S(2)}) collective-permute-start(f32[1,32,128]{2,1,0:T(8,128)S(1)} %get-tuple-element.62), channel_id=1, source_target_pairs={{0,8},{8,16},{16,24},{1,9},{9,17},{17,25},{2,10},{10,18},{18,26},{... | collective-permute-start | bytes 49160 | tf_op jit(solution)/shard_map/ppermute | solution.py:16
  17.4 0.0 collective-permute-done.1
  17.4 2.2 %collective-permute-start = (f32[1,32,128]{2,1,0:T(8,128)S(1)}, f32[1,32,128]{2,1,0:T(8,128)S(1)}, u32[]{:S(2)}, u32[]{:S(2)}) collective-permute-start(f32[1,32,128]{2,1,0:T(8,128)S(1)} %get-tuple-element.59), channel_id=1, source_target_pairs={{8,0},{16,8},{24,16},{9,1},{17,9},{25,17},{10,2},{18,10},{26,18},{... | collective-permute-start | bytes 49160 | tf_op jit(solution)/shard_map/ppermute | solution.py:19
  19.6 0.0 copy-start.2
  19.6 1.0 constant_dynamic-update-slice_fusion.1
  20.7 2.2 %collective-permute-done = f32[1,32,128]{2,1,0:T(8,128)S(1)} collective-permute-done((f32[1,32,128]{2,1,0:T(8,128)S(1)}, f32[1,32,128]{2,1,0:T(8,128)S(1)}, u32[]{:S(2)}, u32[]{:S(2)}) %collective-permute-start) | collective-permute-done | bytes 16416 | tf_op jit(solution)/shard_map/ppermute | solution.py:19
  22.8 6.3 %collective-permute-start.3 = (f32[18,1,128]{2,1,0:T(1,128)S(1)}, f32[18,1,128]{2,1,0:T(1,128)S(1)}, u32[]{:S(2)}, u32[]{:S(2)}) collective-permute-start(f32[18,1,128]{2,1,0:T(1,128)S(1)} %get-tuple-element.47), channel_id=1, source_target_pairs={{0,1},{1,2},{2,3},{3,4},{4,5},{5,6},{6,7},{8,9},{9,10},{10,11},{11... | collective-permute-start | bytes 27656 | tf_op jit(solution)/shard_map/ppermute | solution.py:16
  29.2 0.0 collective-permute-done.17
  29.2 1.9 %collective-permute-start.2 = (f32[18,1,128]{2,1,0:T(1,128)S(1)}, f32[18,1,128]{2,1,0:T(1,128)S(1)}, u32[]{:S(2)}, u32[]{:S(2)}) collective-permute-start(f32[18,1,128]{2,1,0:T(1,128)S(1)} %get-tuple-element.48), channel_id=1, source_target_pairs={{1,0},{2,1},{3,2},{4,3},{5,4},{6,5},{7,6},{9,8},{10,9},{11,10},{12... | collective-permute-start | bytes 27656 | tf_op jit(solution)/shard_map/ppermute | solution.py:19
  31.1 0.0 copy-start.5
  31.2 0.0 collective-permute-done.16
  31.2 1.9 %collective-permute-start.18 = (f32[18,1,128]{2,1,0:T(1,128)S(1)}, f32[18,1,128]{2,1,0:T(1,128)S(1)}, u32[]{:S(2)}, u32[]{:S(2)}) collective-permute-start(f32[18,1,128]{2,1,0:T(1,128)S(1)} %get-tuple-element.49), channel_id=1, source_target_pairs={{1,0},{2,1},{3,2},{4,3},{5,4},{6,5},{7,6},{9,8},{10,9},{11,10},{12... | collective-permute-start | bytes 27656 | tf_op jit(solution)/shard_map/ppermute | solution.py:19
  33.2 3.6 %collective-permute-start.19 = (f32[18,1,128]{2,1,0:T(1,128)S(1)}, f32[18,1,128]{2,1,0:T(1,128)S(1)}, u32[]{:S(2)}, u32[]{:S(2)}) collective-permute-start(f32[18,1,128]{2,1,0:T(1,128)S(1)} %get-tuple-element.50), channel_id=1, source_target_pairs={{0,1},{1,2},{2,3},{3,4},{4,5},{5,6},{6,7},{8,9},{9,10},{10,11},{11... | collective-permute-start | bytes 27656 | tf_op jit(solution)/shard_map/ppermute | solution.py:16
  36.8 0.0 copy-start
  36.8 0.0 copy-start.1
  36.9 2.1 %collective-permute-start.6 = (f32[18,1,128]{2,1,0:T(1,128)S(1)}, f32[18,1,128]{2,1,0:T(1,128)S(1)}, u32[]{:S(2)}, u32[]{:S(2)}) collective-permute-start(f32[18,1,128]{2,1,0:T(1,128)S(1)} %get-tuple-element.45), channel_id=1, source_target_pairs={{1,0},{2,1},{3,2},{4,3},{5,4},{6,5},{7,6},{9,8},{10,9},{11,10},{12... | collective-permute-start | bytes 27656 | tf_op jit(solution)/shard_map/ppermute | solution.py:19
  39.0 0.0 copy-start.6
  39.0 3.8 %collective-permute-start.7 = (f32[18,1,128]{2,1,0:T(1,128)S(1)}, f32[18,1,128]{2,1,0:T(1,128)S(1)}, u32[]{:S(2)}, u32[]{:S(2)}) collective-permute-start(f32[18,1,128]{2,1,0:T(1,128)S(1)} %get-tuple-element.46), channel_id=1, source_target_pairs={{0,1},{1,2},{2,3},{3,4},{4,5},{5,6},{6,7},{8,9},{9,10},{10,11},{11... | collective-permute-start | bytes 27656 | tf_op jit(solution)/shard_map/ppermute | solution.py:16
  42.8 0.0 collective-permute-done.2
  42.8 1.2 multiply_reduce_fusion.1
  44.1 0.4 fusion.26
  44.5 1.9 %collective-permute-start.9 = (f32[1,32,128]{2,1,0:T(8,128)S(1)}, f32[1,32,128]{2,1,0:T(8,128)S(1)}, u32[]{:S(2)}, u32[]{:S(2)}) collective-permute-start(f32[1,32,128]{2,1,0:T(8,128)S(1)} %get-tuple-element.55), channel_id=1, source_target_pairs={{0,8},{8,16},{16,24},{1,9},{9,17},{17,25},{2,10},{10,18},{18,26},{... | collective-permute-start | bytes 49160 | tf_op jit(solution)/shard_map/ppermute | solution.py:16
  46.4 3.4 %collective-permute-start.8 = (f32[1,32,128]{2,1,0:T(8,128)S(1)}, f32[1,32,128]{2,1,0:T(8,128)S(1)}, u32[]{:S(2)}, u32[]{:S(2)}) collective-permute-start(f32[1,32,128]{2,1,0:T(8,128)S(1)} %get-tuple-element.56), channel_id=1, source_target_pairs={{8,0},{16,8},{24,16},{9,1},{17,9},{25,17},{10,2},{18,10},{26,18},{... | collective-permute-start | bytes 49160 | tf_op jit(solution)/shard_map/ppermute | solution.py:19
  49.8 2.0 %collective-permute-done.8 = f32[1,32,128]{2,1,0:T(8,128)S(1)} collective-permute-done((f32[1,32,128]{2,1,0:T(8,128)S(1)}, f32[1,32,128]{2,1,0:T(8,128)S(1)}, u32[]{:S(2)}, u32[]{:S(2)}) %collective-permute-start.8) | collective-permute-done | bytes 16416 | tf_op jit(solution)/shard_map/ppermute | solution.py:19
  51.8 1.9 %collective-permute-start.10 = (f32[18,1,128]{2,1,0:T(1,128)S(1)}, f32[18,1,128]{2,1,0:T(1,128)S(1)}, u32[]{:S(2)}, u32[]{:S(2)}) collective-permute-start(f32[18,1,128]{2,1,0:T(1,128)S(1)} %get-tuple-element.43), channel_id=1, source_target_pairs={{1,0},{2,1},{3,2},{4,3},{5,4},{6,5},{7,6},{9,8},{10,9},{11,10},{12... | collective-permute-start | bytes 27656 | tf_op jit(solution)/shard_map/ppermute | solution.py:19
  53.8 4.8 %collective-permute-start.11 = (f32[18,1,128]{2,1,0:T(1,128)S(1)}, f32[18,1,128]{2,1,0:T(1,128)S(1)}, u32[]{:S(2)}, u32[]{:S(2)}) collective-permute-start(f32[18,1,128]{2,1,0:T(1,128)S(1)} %get-tuple-element.44), channel_id=1, source_target_pairs={{0,1},{1,2},{2,3},{3,4},{4,5},{5,6},{6,7},{8,9},{9,10},{10,11},{11... | collective-permute-start | bytes 27656 | tf_op jit(solution)/shard_map/ppermute | solution.py:16
  58.6 0.8 collective-permute-done.11
  59.4 1.0 multiply_reduce_fusion.4
  60.4 14.9 %all-reduce.9 = (f32[]{:T(128)}, f32[]{:T(128)}, f32[]{:T(128)}, f32[]{:T(128)}) all-reduce(f32[]{:T(128)} %get-tuple-element.6, f32[]{:T(128)} %get-tuple-element.5, f32[]{:T(128)} %get-tuple-element.4, f32[]{:T(128)} %get-tuple-element.3), channel_id=1, replica_groups=mesh['gy'=4,'gz'=8] {'gz'}, use_global_device_ids=true, to_apply=%region_1.2 | all-reduce | flops 4 | bytes 32 | tf_op jit(solution)/shard_map/psum | solution.py:77
  75.4 7.5 %all-reduce.11 = (f32[]{:T(128)}, f32[]{:T(128)}, f32[]{:T(128)}, f32[]{:T(128)}) all-reduce(f32[]{:T(128)} %get-tuple-element.11, f32[]{:T(128)} %get-tuple-element.12, f32[]{:T(128)} %get-tuple-element.13, f32[]{:T(128)} %get-tuple-element.14), channel_id=1, replica_groups=mesh['gy'=4,'gz'=8] {'gy'}, use_global_device_ids=true, to_apply=%region_2.3 | all-reduce | flops 4 | bytes 32 | tf_op jit(solution)/shard_map/psum | solution.py:77
  84.2 0.7 multiply_reduce_fusion
  84.9 0.6 fusion.107
  85.5 3.2 %collective-permute-start.21 = (f32[1,32,128]{2,1,0:T(8,128)}, f32[1,32,128]{2,1,0:T(8,128)S(1)}, u32[]{:S(2)}, u32[]{:S(2)}) collective-permute-start(f32[1,32,128]{2,1,0:T(8,128)} %get-tuple-element.51), channel_id=1, source_target_pairs={{0,8},{8,16},{16,24},{1,9},{9,17},{17,25},{2,10},{10,18},{18,26},{... | collective-permute-start | bytes 49160 | tf_op jit(solution)/shard_map/ppermute | solution.py:16
  88.7 2.1 %collective-permute-start.20 = (f32[1,32,128]{2,1,0:T(8,128)S(1)}, f32[1,32,128]{2,1,0:T(8,128)S(1)}, u32[]{:S(2)}, u32[]{:S(2)}) collective-permute-start(f32[1,32,128]{2,1,0:T(8,128)S(1)} %get-tuple-element.52), channel_id=1, source_target_pairs={{8,0},{16,8},{24,16},{9,1},{17,9},{25,17},{10,2},{18,10},{26,18},{... | collective-permute-start | bytes 49160 | tf_op jit(solution)/shard_map/ppermute | solution.py:19
  92.1 0.8 multiply_reduce_fusion.3
  92.9 4.1 %collective-permute-start.13 = (f32[1,32,128]{2,1,0:T(8,128)S(1)}, f32[1,32,128]{2,1,0:T(8,128)S(1)}, u32[]{:S(2)}, u32[]{:S(2)}) collective-permute-start(f32[1,32,128]{2,1,0:T(8,128)S(1)} %get-tuple-element.53), channel_id=1, source_target_pairs={{0,8},{8,16},{16,24},{1,9},{9,17},{17,25},{2,10},{10,18},{18,26},{... | collective-permute-start | bytes 49160 | tf_op jit(solution)/shard_map/ppermute | solution.py:16
  96.9 1.9 %collective-permute-start.12 = (f32[1,32,128]{2,1,0:T(8,128)S(1)}, f32[1,32,128]{2,1,0:T(8,128)S(1)}, u32[]{:S(2)}, u32[]{:S(2)}) collective-permute-start(f32[1,32,128]{2,1,0:T(8,128)S(1)} %get-tuple-element.54), channel_id=1, source_target_pairs={{8,0},{16,8},{24,16},{9,1},{17,9},{25,17},{10,2},{18,10},{26,18},{... | collective-permute-start | bytes 49160 | tf_op jit(solution)/shard_map/ppermute | solution.py:19
  98.9 7.0 %collective-permute-start.22 = (f32[18,1,128]{2,1,0:T(1,128)S(1)}, f32[18,1,128]{2,1,0:T(1,128)S(1)}, u32[]{:S(2)}, u32[]{:S(2)}) collective-permute-start(f32[18,1,128]{2,1,0:T(1,128)S(1)} %get-tuple-element.39), channel_id=1, source_target_pairs={{1,0},{2,1},{3,2},{4,3},{5,4},{6,5},{7,6},{9,8},{10,9},{11,10},{12... | collective-permute-start | bytes 27656 | tf_op jit(solution)/shard_map/ppermute | solution.py:19
  105.9 1.9 %collective-permute-start.23 = (f32[18,1,128]{2,1,0:T(1,128)S(1)}, f32[18,1,128]{2,1,0:T(1,128)S(1)}, u32[]{:S(2)}, u32[]{:S(2)}) collective-permute-start(f32[18,1,128]{2,1,0:T(1,128)S(1)} %get-tuple-element.40), channel_id=1, source_target_pairs={{0,1},{1,2},{2,3},{3,4},{4,5},{5,6},{6,7},{8,9},{9,10},{10,11},{11... | collective-permute-start | bytes 27656 | tf_op jit(solution)/shard_map/ppermute | solution.py:16
  107.9 2.6 %collective-permute-start.14 = (f32[18,1,128]{2,1,0:T(1,128)S(1)}, f32[18,1,128]{2,1,0:T(1,128)S(1)}, u32[]{:S(2)}, u32[]{:S(2)}) collective-permute-start(f32[18,1,128]{2,1,0:T(1,128)S(1)} %get-tuple-element.41), channel_id=1, source_target_pairs={{1,0},{2,1},{3,2},{4,3},{5,4},{6,5},{7,6},{9,8},{10,9},{11,10},{12... | collective-permute-start | bytes 27656 | tf_op jit(solution)/shard_map/ppermute | solution.py:19
  110.5 3.0 %collective-permute-start.15 = (f32[18,1,128]{2,1,0:T(1,128)S(1)}, f32[18,1,128]{2,1,0:T(1,128)S(1)}, u32[]{:S(2)}, u32[]{:S(2)}) collective-permute-start(f32[18,1,128]{2,1,0:T(1,128)S(1)} %get-tuple-element.42), channel_id=1, source_target_pairs={{0,1},{1,2},{2,3},{3,4},{4,5},{5,6},{6,7},{8,9},{9,10},{10,11},{11... | collective-permute-start | bytes 27656 | tf_op jit(solution)/shard_map/ppermute | solution.py:16
  113.5 1.0 fusion.46
  114.5 1.0 fusion.36
  115.5 13.1 %all-reduce.8 = (f32[]{:T(128)}, f32[]{:T(128)}, f32[]{:T(128)}, f32[]{:T(128)}) all-reduce(f32[]{:T(128)} %get-tuple-element.25, f32[]{:T(128)} %fusion.36, f32[]{:T(128)} %get-tuple-element.23, f32[]{:T(128)} %fusion.46), channel_id=1, replica_groups=mesh['gy'=4,'gz'=8] {'gz'}, use_global_device_ids=true, to_apply=%region_7.8 | all-reduce | flops 4 | bytes 32 | tf_op jit(solution)/shard_map/psum | solution.py:77
  128.6 8.0 %all-reduce.10 = (f32[]{:T(128)}, f32[]{:T(128)}, f32[]{:T(128)}, f32[]{:T(128)}) all-reduce(f32[]{:T(128)} %get-tuple-element.7, f32[]{:T(128)} %get-tuple-element.8, f32[]{:T(128)} %get-tuple-element.9, f32[]{:T(128)} %get-tuple-element.10), channel_id=1, replica_groups=mesh['gy'=4,'gz'=8] {'gy'}, use_global_device_ids=true, to_apply=%region_8.9 | all-reduce | flops 4 | bytes 32 | tf_op jit(solution)/shard_map/psum | solution.py:77
  145.9 0.1 multiply_add_fusion
  146.0 0.0 copy-start.3
  146.0 0.0 copy-start.4
  146.1 2.8 %collective-permute-start.24 = (f32[2,1,32,128]{3,2,1,0:T(8,128)S(1)}, f32[2,1,32,128]{3,2,1,0:T(8,128)S(1)}, u32[]{:S(2)}, u32[]{:S(2)}) collective-permute-start(f32[2,1,32,128]{3,2,1,0:T(8,128)S(1)} %get-tuple-element.37), channel_id=1, source_target_pairs={{0,8},{8,16},{16,24},{1,9},{9,17},{17,25},{2,10},{10,18},{18,26},{... | collective-permute-start | bytes 98312 | tf_op jit(solution)/shard_map/ppermute | solution.py:16
  148.9 2.5 %collective-permute-start.25 = (f32[2,1,32,128]{3,2,1,0:T(8,128)S(1)}, f32[2,1,32,128]{3,2,1,0:T(8,128)S(1)}, u32[]{:S(2)}, u32[]{:S(2)}) collective-permute-start(f32[2,1,32,128]{3,2,1,0:T(8,128)S(1)} %get-tuple-element.38), channel_id=1, source_target_pairs={{8,0},{16,8},{24,16},{9,1},{17,9},{25,17},{10,2},{18,10},{26,18},{... | collective-permute-start | bytes 98312 | tf_op jit(solution)/shard_map/ppermute | solution.py:19
  151.4 3.1 %collective-permute-done.25 = f32[2,1,32,128]{3,2,1,0:T(8,128)S(1)} collective-permute-done((f32[2,1,32,128]{3,2,1,0:T(8,128)S(1)}, f32[2,1,32,128]{3,2,1,0:T(8,128)S(1)}, u32[]{:S(2)}, u32[]{:S(2)}) %collective-permute-start.25) | collective-permute-done | bytes 32800 | tf_op jit(solution)/shard_map/ppermute | solution.py:19
  154.5 5.2 %collective-permute-start.26 = (f32[2,18,1,128]{3,2,1,0:T(1,128)S(1)}, f32[2,18,1,128]{3,2,1,0:T(1,128)S(1)}, u32[]{:S(2)}, u32[]{:S(2)}) collective-permute-start(f32[2,18,1,128]{3,2,1,0:T(1,128)S(1)} %get-tuple-element.35), channel_id=1, source_target_pairs={{0,1},{1,2},{2,3},{3,4},{4,5},{5,6},{6,7},{8,9},{9,10},{10,11},{11... | collective-permute-start | bytes 55304 | tf_op jit(solution)/shard_map/ppermute | solution.py:16
  159.7 3.1 %collective-permute-start.27 = (f32[2,18,1,128]{3,2,1,0:T(1,128)S(1)}, f32[2,18,1,128]{3,2,1,0:T(1,128)S(1)}, u32[]{:S(2)}, u32[]{:S(2)}) collective-permute-start(f32[2,18,1,128]{3,2,1,0:T(1,128)S(1)} %get-tuple-element.36), channel_id=1, source_target_pairs={{1,0},{2,1},{3,2},{4,3},{5,4},{6,5},{7,6},{9,8},{10,9},{11,10},{12... | collective-permute-start | bytes 55304 | tf_op jit(solution)/shard_map/ppermute | solution.py:19
  162.8 2.0 %collective-permute-done.27 = f32[2,18,1,128]{3,2,1,0:T(1,128)S(1)} collective-permute-done((f32[2,18,1,128]{3,2,1,0:T(1,128)S(1)}, f32[2,18,1,128]{3,2,1,0:T(1,128)S(1)}, u32[]{:S(2)}, u32[]{:S(2)}) %collective-permute-start.27) | collective-permute-done | bytes 18464 | tf_op jit(solution)/shard_map/ppermute | solution.py:19
  164.8 0.1 pad_maximum_fusion
  164.9 0.1 slice_bitcast_fusion
  165.0 1.4 fusion.7
  (46 shorter events, 0.3 us)
Async XLA Ops:
  1.4 35.5 %collective-permute-start.4 = (f32[1,32,128]{2,1,0:T(8,128)S(1)}, f32[1,32,128]{2,1,0:T(8,128)S(1)}, u32[]{:S(2)}, u32[]{:S(2)}) collective-permute-start(f32[1,32,128]{2,1,0:T(8,128)S(1)} %get-tuple-element.57), channel_id=1, source_target_pairs={{8,0},{16,8},{24,16},{9,1},{17,9},{25,17},{10,2},{18,10},{26,18},{... | collective-permute-start | bytes 49160 | tf_op jit(solution)/shard_map/ppermute | solution.py:19
  3.3 29.9 %collective-permute-start.5 = (f32[1,32,128]{2,1,0:T(8,128)S(1)}, f32[1,32,128]{2,1,0:T(8,128)S(1)}, u32[]{:S(2)}, u32[]{:S(2)}) collective-permute-start(f32[1,32,128]{2,1,0:T(8,128)S(1)} %get-tuple-element.58), channel_id=1, source_target_pairs={{0,8},{8,16},{16,24},{1,9},{9,17},{17,25},{2,10},{10,18},{18,26},{... | collective-permute-start | bytes 49160 | tf_op jit(solution)/shard_map/ppermute | solution.py:16
  8.3 9.1 %collective-permute-start.1 = (f32[1,32,128]{2,1,0:T(8,128)S(1)}, f32[1,32,128]{2,1,0:T(8,128)S(1)}, u32[]{:S(2)}, u32[]{:S(2)}) collective-permute-start(f32[1,32,128]{2,1,0:T(8,128)S(1)} %get-tuple-element.60), channel_id=1, source_target_pairs={{0,8},{8,16},{16,24},{1,9},{9,17},{17,25},{2,10},{10,18},{18,26},{... | collective-permute-start | bytes 49160 | tf_op jit(solution)/shard_map/ppermute | solution.py:16
  11.2 19.9 %collective-permute-start.16 = (f32[1,32,128]{2,1,0:T(8,128)S(1)}, f32[1,32,128]{2,1,0:T(8,128)S(1)}, u32[]{:S(2)}, u32[]{:S(2)}) collective-permute-start(f32[1,32,128]{2,1,0:T(8,128)S(1)} %get-tuple-element.61), channel_id=1, source_target_pairs={{8,0},{16,8},{24,16},{9,1},{17,9},{25,17},{10,2},{18,10},{26,18},{... | collective-permute-start | bytes 49160 | tf_op jit(solution)/shard_map/ppermute | solution.py:19
  14.3 14.9 %collective-permute-start.17 = (f32[1,32,128]{2,1,0:T(8,128)S(1)}, f32[1,32,128]{2,1,0:T(8,128)S(1)}, u32[]{:S(2)}, u32[]{:S(2)}) collective-permute-start(f32[1,32,128]{2,1,0:T(8,128)S(1)} %get-tuple-element.62), channel_id=1, source_target_pairs={{0,8},{8,16},{16,24},{1,9},{9,17},{17,25},{2,10},{10,18},{18,26},{... | collective-permute-start | bytes 49160 | tf_op jit(solution)/shard_map/ppermute | solution.py:16
  17.4 5.4 %collective-permute-start = (f32[1,32,128]{2,1,0:T(8,128)S(1)}, f32[1,32,128]{2,1,0:T(8,128)S(1)}, u32[]{:S(2)}, u32[]{:S(2)}) collective-permute-start(f32[1,32,128]{2,1,0:T(8,128)S(1)} %get-tuple-element.59), channel_id=1, source_target_pairs={{8,0},{16,8},{24,16},{9,1},{17,9},{25,17},{10,2},{18,10},{26,18},{... | collective-permute-start | bytes 49160 | tf_op jit(solution)/shard_map/ppermute | solution.py:19
  19.6 11.5 %copy-start.2 = (f32[16,32,128]{2,1,0:T(8,128)S(1)}, f32[16,32,128]{2,1,0:T(8,128)}, u32[]{:S(2)}) copy-start(f32[16,32,128]{2,1,0:T(8,128)} %param.9) | copy-start | bytes 786436
  22.8 16.1 %collective-permute-start.3 = (f32[18,1,128]{2,1,0:T(1,128)S(1)}, f32[18,1,128]{2,1,0:T(1,128)S(1)}, u32[]{:S(2)}, u32[]{:S(2)}) collective-permute-start(f32[18,1,128]{2,1,0:T(1,128)S(1)} %get-tuple-element.47), channel_id=1, source_target_pairs={{0,1},{1,2},{2,3},{3,4},{4,5},{5,6},{6,7},{8,9},{9,10},{10,11},{11... | collective-permute-start | bytes 27656 | tf_op jit(solution)/shard_map/ppermute | solution.py:16
  29.2 13.6 %collective-permute-start.2 = (f32[18,1,128]{2,1,0:T(1,128)S(1)}, f32[18,1,128]{2,1,0:T(1,128)S(1)}, u32[]{:S(2)}, u32[]{:S(2)}) collective-permute-start(f32[18,1,128]{2,1,0:T(1,128)S(1)} %get-tuple-element.48), channel_id=1, source_target_pairs={{1,0},{2,1},{3,2},{4,3},{5,4},{6,5},{7,6},{9,8},{10,9},{11,10},{12... | collective-permute-start | bytes 27656 | tf_op jit(solution)/shard_map/ppermute | solution.py:19
  31.1 5.7 %copy-start.5 = (f32[16,32,128]{2,1,0:T(8,128)S(1)}, f32[16,32,128]{2,1,0:T(8,128)}, u32[]{:S(2)}) copy-start(f32[16,32,128]{2,1,0:T(8,128)} %param.8) | copy-start | bytes 786436
  31.2 11.6 %collective-permute-start.18 = (f32[18,1,128]{2,1,0:T(1,128)S(1)}, f32[18,1,128]{2,1,0:T(1,128)S(1)}, u32[]{:S(2)}, u32[]{:S(2)}) collective-permute-start(f32[18,1,128]{2,1,0:T(1,128)S(1)} %get-tuple-element.49), channel_id=1, source_target_pairs={{1,0},{2,1},{3,2},{4,3},{5,4},{6,5},{7,6},{9,8},{10,9},{11,10},{12... | collective-permute-start | bytes 27656 | tf_op jit(solution)/shard_map/ppermute | solution.py:19
  33.2 9.7 %collective-permute-start.19 = (f32[18,1,128]{2,1,0:T(1,128)S(1)}, f32[18,1,128]{2,1,0:T(1,128)S(1)}, u32[]{:S(2)}, u32[]{:S(2)}) collective-permute-start(f32[18,1,128]{2,1,0:T(1,128)S(1)} %get-tuple-element.50), channel_id=1, source_target_pairs={{0,1},{1,2},{2,3},{3,4},{4,5},{5,6},{6,7},{8,9},{9,10},{10,11},{11... | collective-permute-start | bytes 27656 | tf_op jit(solution)/shard_map/ppermute | solution.py:16
  36.8 6.0 %copy-start = (f32[16,32,128]{2,1,0:T(8,128)S(1)}, f32[16,32,128]{2,1,0:T(8,128)}, u32[]{:S(2)}) copy-start(f32[16,32,128]{2,1,0:T(8,128)} %param.5) | copy-start | bytes 786436
  36.8 6.0 %copy-start.1 = (s32[16,32,128]{2,1,0:T(8,128)S(1)}, s32[16,32,128]{2,1,0:T(8,128)}, u32[]{:S(2)}) copy-start(s32[16,32,128]{2,1,0:T(8,128)} %param.6) | copy-start | bytes 786436
  36.9 7.2 %collective-permute-start.6 = (f32[18,1,128]{2,1,0:T(1,128)S(1)}, f32[18,1,128]{2,1,0:T(1,128)S(1)}, u32[]{:S(2)}, u32[]{:S(2)}) collective-permute-start(f32[18,1,128]{2,1,0:T(1,128)S(1)} %get-tuple-element.45), channel_id=1, source_target_pairs={{1,0},{2,1},{3,2},{4,3},{5,4},{6,5},{7,6},{9,8},{10,9},{11,10},{12... | collective-permute-start | bytes 27656 | tf_op jit(solution)/shard_map/ppermute | solution.py:19
  39.0 5.1 %copy-start.6 = (s32[16,32,128]{2,1,0:T(8,128)S(1)}, s32[16,32,128]{2,1,0:T(8,128)}, u32[]{:S(2)}) copy-start(s32[16,32,128]{2,1,0:T(8,128)} %param.7) | copy-start | bytes 786436
  39.0 5.1 %collective-permute-start.7 = (f32[18,1,128]{2,1,0:T(1,128)S(1)}, f32[18,1,128]{2,1,0:T(1,128)S(1)}, u32[]{:S(2)}, u32[]{:S(2)}) collective-permute-start(f32[18,1,128]{2,1,0:T(1,128)S(1)} %get-tuple-element.46), channel_id=1, source_target_pairs={{0,1},{1,2},{2,3},{3,4},{4,5},{5,6},{6,7},{8,9},{9,10},{10,11},{11... | collective-permute-start | bytes 27656 | tf_op jit(solution)/shard_map/ppermute | solution.py:16
  44.5 5.3 %collective-permute-start.9 = (f32[1,32,128]{2,1,0:T(8,128)S(1)}, f32[1,32,128]{2,1,0:T(8,128)S(1)}, u32[]{:S(2)}, u32[]{:S(2)}) collective-permute-start(f32[1,32,128]{2,1,0:T(8,128)S(1)} %get-tuple-element.55), channel_id=1, source_target_pairs={{0,8},{8,16},{16,24},{1,9},{9,17},{17,25},{2,10},{10,18},{18,26},{... | collective-permute-start | bytes 49160 | tf_op jit(solution)/shard_map/ppermute | solution.py:16
  46.4 5.4 %collective-permute-start.8 = (f32[1,32,128]{2,1,0:T(8,128)S(1)}, f32[1,32,128]{2,1,0:T(8,128)S(1)}, u32[]{:S(2)}, u32[]{:S(2)}) collective-permute-start(f32[1,32,128]{2,1,0:T(8,128)S(1)} %get-tuple-element.56), channel_id=1, source_target_pairs={{8,0},{16,8},{24,16},{9,1},{17,9},{25,17},{10,2},{18,10},{26,18},{... | collective-permute-start | bytes 49160 | tf_op jit(solution)/shard_map/ppermute | solution.py:19
  51.8 6.8 %collective-permute-start.10 = (f32[18,1,128]{2,1,0:T(1,128)S(1)}, f32[18,1,128]{2,1,0:T(1,128)S(1)}, u32[]{:S(2)}, u32[]{:S(2)}) collective-permute-start(f32[18,1,128]{2,1,0:T(1,128)S(1)} %get-tuple-element.43), channel_id=1, source_target_pairs={{1,0},{2,1},{3,2},{4,3},{5,4},{6,5},{7,6},{9,8},{10,9},{11,10},{12... | collective-permute-start | bytes 27656 | tf_op jit(solution)/shard_map/ppermute | solution.py:19
  53.8 5.6 %collective-permute-start.11 = (f32[18,1,128]{2,1,0:T(1,128)S(1)}, f32[18,1,128]{2,1,0:T(1,128)S(1)}, u32[]{:S(2)}, u32[]{:S(2)}) collective-permute-start(f32[18,1,128]{2,1,0:T(1,128)S(1)} %get-tuple-element.44), channel_id=1, source_target_pairs={{0,1},{1,2},{2,3},{3,4},{4,5},{5,6},{6,7},{8,9},{9,10},{10,11},{11... | collective-permute-start | bytes 27656 | tf_op jit(solution)/shard_map/ppermute | solution.py:16
  85.5 13.3 %collective-permute-start.21 = (f32[1,32,128]{2,1,0:T(8,128)}, f32[1,32,128]{2,1,0:T(8,128)S(1)}, u32[]{:S(2)}, u32[]{:S(2)}) collective-permute-start(f32[1,32,128]{2,1,0:T(8,128)} %get-tuple-element.51), channel_id=1, source_target_pairs={{0,8},{8,16},{16,24},{1,9},{9,17},{17,25},{2,10},{10,18},{18,26},{... | collective-permute-start | bytes 49160 | tf_op jit(solution)/shard_map/ppermute | solution.py:16
  88.7 10.2 %collective-permute-start.20 = (f32[1,32,128]{2,1,0:T(8,128)S(1)}, f32[1,32,128]{2,1,0:T(8,128)S(1)}, u32[]{:S(2)}, u32[]{:S(2)}) collective-permute-start(f32[1,32,128]{2,1,0:T(8,128)S(1)} %get-tuple-element.52), channel_id=1, source_target_pairs={{8,0},{16,8},{24,16},{9,1},{17,9},{25,17},{10,2},{18,10},{26,18},{... | collective-permute-start | bytes 49160 | tf_op jit(solution)/shard_map/ppermute | solution.py:19
  92.9 15.0 %collective-permute-start.13 = (f32[1,32,128]{2,1,0:T(8,128)S(1)}, f32[1,32,128]{2,1,0:T(8,128)S(1)}, u32[]{:S(2)}, u32[]{:S(2)}) collective-permute-start(f32[1,32,128]{2,1,0:T(8,128)S(1)} %get-tuple-element.53), channel_id=1, source_target_pairs={{0,8},{8,16},{16,24},{1,9},{9,17},{17,25},{2,10},{10,18},{18,26},{... | collective-permute-start | bytes 49160 | tf_op jit(solution)/shard_map/ppermute | solution.py:16
  96.9 10.9 %collective-permute-start.12 = (f32[1,32,128]{2,1,0:T(8,128)S(1)}, f32[1,32,128]{2,1,0:T(8,128)S(1)}, u32[]{:S(2)}, u32[]{:S(2)}) collective-permute-start(f32[1,32,128]{2,1,0:T(8,128)S(1)} %get-tuple-element.54), channel_id=1, source_target_pairs={{8,0},{16,8},{24,16},{9,1},{17,9},{25,17},{10,2},{18,10},{26,18},{... | collective-permute-start | bytes 49160 | tf_op jit(solution)/shard_map/ppermute | solution.py:19
  98.9 14.6 %collective-permute-start.22 = (f32[18,1,128]{2,1,0:T(1,128)S(1)}, f32[18,1,128]{2,1,0:T(1,128)S(1)}, u32[]{:S(2)}, u32[]{:S(2)}) collective-permute-start(f32[18,1,128]{2,1,0:T(1,128)S(1)} %get-tuple-element.39), channel_id=1, source_target_pairs={{1,0},{2,1},{3,2},{4,3},{5,4},{6,5},{7,6},{9,8},{10,9},{11,10},{12... | collective-permute-start | bytes 27656 | tf_op jit(solution)/shard_map/ppermute | solution.py:19
  105.9 7.6 %collective-permute-start.23 = (f32[18,1,128]{2,1,0:T(1,128)S(1)}, f32[18,1,128]{2,1,0:T(1,128)S(1)}, u32[]{:S(2)}, u32[]{:S(2)}) collective-permute-start(f32[18,1,128]{2,1,0:T(1,128)S(1)} %get-tuple-element.40), channel_id=1, source_target_pairs={{0,1},{1,2},{2,3},{3,4},{4,5},{5,6},{6,7},{8,9},{9,10},{10,11},{11... | collective-permute-start | bytes 27656 | tf_op jit(solution)/shard_map/ppermute | solution.py:16
  107.9 6.6 %collective-permute-start.14 = (f32[18,1,128]{2,1,0:T(1,128)S(1)}, f32[18,1,128]{2,1,0:T(1,128)S(1)}, u32[]{:S(2)}, u32[]{:S(2)}) collective-permute-start(f32[18,1,128]{2,1,0:T(1,128)S(1)} %get-tuple-element.41), channel_id=1, source_target_pairs={{1,0},{2,1},{3,2},{4,3},{5,4},{6,5},{7,6},{9,8},{10,9},{11,10},{12... | collective-permute-start | bytes 27656 | tf_op jit(solution)/shard_map/ppermute | solution.py:19
  110.5 4.0 %collective-permute-start.15 = (f32[18,1,128]{2,1,0:T(1,128)S(1)}, f32[18,1,128]{2,1,0:T(1,128)S(1)}, u32[]{:S(2)}, u32[]{:S(2)}) collective-permute-start(f32[18,1,128]{2,1,0:T(1,128)S(1)} %get-tuple-element.42), channel_id=1, source_target_pairs={{0,1},{1,2},{2,3},{3,4},{4,5},{5,6},{6,7},{8,9},{9,10},{10,11},{11... | collective-permute-start | bytes 27656 | tf_op jit(solution)/shard_map/ppermute | solution.py:16
  146.0 18.8 %copy-start.3 = (f32[16,32,128]{2,1,0:T(8,128)}, f32[16,32,128]{2,1,0:T(8,128)S(1)}, u32[]{:S(2)}) copy-start(f32[16,32,128]{2,1,0:T(8,128)S(1)} %get-tuple-element.63) | copy-start | bytes 786436
  146.0 18.7 %copy-start.4 = (f32[16,32,128]{2,1,0:T(8,128)}, f32[16,32,128]{2,1,0:T(8,128)S(1)}, u32[]{:S(2)}) copy-start(f32[16,32,128]{2,1,0:T(8,128)S(1)} %get-tuple-element.64) | copy-start | bytes 786436
  146.1 5.3 %collective-permute-start.24 = (f32[2,1,32,128]{3,2,1,0:T(8,128)S(1)}, f32[2,1,32,128]{3,2,1,0:T(8,128)S(1)}, u32[]{:S(2)}, u32[]{:S(2)}) collective-permute-start(f32[2,1,32,128]{3,2,1,0:T(8,128)S(1)} %get-tuple-element.37), channel_id=1, source_target_pairs={{0,8},{8,16},{16,24},{1,9},{9,17},{17,25},{2,10},{10,18},{18,26},{... | collective-permute-start | bytes 98312 | tf_op jit(solution)/shard_map/ppermute | solution.py:16
  148.9 5.6 %collective-permute-start.25 = (f32[2,1,32,128]{3,2,1,0:T(8,128)S(1)}, f32[2,1,32,128]{3,2,1,0:T(8,128)S(1)}, u32[]{:S(2)}, u32[]{:S(2)}) collective-permute-start(f32[2,1,32,128]{3,2,1,0:T(8,128)S(1)} %get-tuple-element.38), channel_id=1, source_target_pairs={{8,0},{16,8},{24,16},{9,1},{17,9},{25,17},{10,2},{18,10},{26,18},{... | collective-permute-start | bytes 98312 | tf_op jit(solution)/shard_map/ppermute | solution.py:19
  154.5 8.3 %collective-permute-start.26 = (f32[2,18,1,128]{3,2,1,0:T(1,128)S(1)}, f32[2,18,1,128]{3,2,1,0:T(1,128)S(1)}, u32[]{:S(2)}, u32[]{:S(2)}) collective-permute-start(f32[2,18,1,128]{3,2,1,0:T(1,128)S(1)} %get-tuple-element.35), channel_id=1, source_target_pairs={{0,1},{1,2},{2,3},{3,4},{4,5},{5,6},{6,7},{8,9},{9,10},{10,11},{11... | collective-permute-start | bytes 55304 | tf_op jit(solution)/shard_map/ppermute | solution.py:16
  159.7 5.1 %collective-permute-start.27 = (f32[2,18,1,128]{3,2,1,0:T(1,128)S(1)}, f32[2,18,1,128]{3,2,1,0:T(1,128)S(1)}, u32[]{:S(2)}, u32[]{:S(2)}) collective-permute-start(f32[2,18,1,128]{3,2,1,0:T(1,128)S(1)} %get-tuple-element.36), channel_id=1, source_target_pairs={{1,0},{2,1},{3,2},{4,3},{5,4},{6,5},{7,6},{9,8},{10,9},{11,10},{12... | collective-permute-start | bytes 55304 | tf_op jit(solution)/shard_map/ppermute | solution.py:19
